TPU v7x, 256 devices: a whole 4x4x8 slice. The times are simulated.
256 devices in a mesh: gx: 32 (over x, y, core), gy: 8 (over z).
Axes of the slice: x: 4, y: 4, z: 8, core: 2. Of those that a mesh axis runs over, the one named last changes fastest.
Arguments:
- leaf_maps: float32 [32, 8, 1024, 1024], P('gx', 'gy'), may hold values from -8 to 40, as said below
- edge_data: float32 [32, 8, 512, 1024], P('gx', 'gy'), may hold values from -6 to 6
Outputs:
- potential: float32 [32, 8, 1024, 1024], P('gx', 'gy')
- flux: float32 [32, 8, 1024, 1024], P('gx', 'gy')
Inputs may be any that keep to these rules, and one draw needn't show every extreme that they name: `leaf_maps`: each leaf's map is exactly symmetric and positive definite.
All inputs are finite; a program needn't handle non-finite values.
Results may differ from a plain program's by a relative error of at most 0.0003.
Values sent between devices are 32-bit elements; how exact they have to be, the bound alone decides.
A program may use at most 128 MiB of HBM per device.

v0:
```python
import jax
import jax.numpy as jnp
from jax import lax
from jax.experimental import pallas as pl
from jax.experimental.pallas import tpu as pltpu
from jax.sharding import PartitionSpec as P

F32 = jnp.float32
BF = jnp.bfloat16


def dot(a, b, dims=((1,), (0,))):
    return lax.dot_general(
        a, b, (dims, ((), ())), precision=lax.Precision.HIGHEST, preferred_element_type=F32
    )


def split(v):
    hi = v.astype(BF)
    return hi, (v - hi.astype(F32)).astype(BF)


def dot3(a, b):
    mm = lambda x, y: jnp.dot(x, y, preferred_element_type=F32)
    return mm(a[0], b[0]) + (mm(a[0], b[1]) + mm(a[1], b[0]))


def sub_bcast(v, i):
    return jnp.broadcast_to(v[i : i + 1, :], v.shape)


def lane_bcast(v, j):
    return jnp.broadcast_to(v[:, j : j + 1], v.shape)


def invert_tiles(tiles):
    lane = lax.broadcasted_iota(jnp.int32, (8, 128), 1)
    subl = lax.broadcasted_iota(jnp.int32, (8, 128), 0)
    tiles = [list(t) for t in tiles]
    count = len(tiles[0])
    left = [[] for _ in tiles]
    right = [[] for _ in tiles]
    for k in range(count):
        base = 8 * k
        inside = (lane >= base) & (lane < base + 8)
        seen = lane < base + 8
        eye = jnp.where(lane - base == subl, 1.0, 0.0)
        for ti, rows in enumerate(tiles):
            pan = rows[k]
            cols = [lane_bcast(pan, base + j) for j in range(8)]
            a = [[sub_bcast(cols[j], i) if i >= j else None for j in range(8)] for i in range(8)]
            seeded = jnp.where(inside, eye, pan)
            left[ti].append(jnp.where(seen, seeded, 0.0))
            r = [sub_bcast(seeded, i) for i in range(8)]
            l = [[None] * 8 for _ in range(8)]
            inv = [None] * 8
            for j in range(8):
                if j % 2 == 0:
                    inv[j] = 1.0 / a[j][j]
                    det = a[j][j] * a[j + 1][j + 1] - a[j + 1][j] * a[j + 1][j]
                    inv[j + 1] = a[j][j] * (1.0 / det)
                for i in range(j + 1, 8):
                    l[i][j] = a[i][j] * inv[j]
                for i in range(j + 1, 8):
                    for q in range(j + 1, i + 1):
                        a[i][q] = a[i][q] - l[i][j] * a[q][j]
            for j in range(8):
                for i in range(j + 1, 8):
                    r[i] = r[i] - l[i][j] * r[j]
            for j in range(8):
                r[j] = r[j] * inv[j]
            for j in range(7, 0, -1):
                for i in range(j):
                    r[i] = r[i] - l[j][i] * r[j]
            out = r[0]
            for i in range(1, 8):
                out = jnp.where(subl == i, r[i], out)
            right[ti].append(jnp.where(seen, out, 0.0))
            for m in range(k + 1, count):
                v = rows[m]
                acc = jnp.where(inside, 0.0, v)
                p = [lane_bcast(v, base + j) * r[j] for j in range(8)]
                rows[m] = acc - (((p[0] + p[1]) + (p[2] + p[3])) + ((p[4] + p[5]) + (p[6] + p[7])))
    return [
        dot(jnp.concatenate(x, 0), jnp.concatenate(y, 0), ((0,), (0,)))
        for x, y in zip(left, right)
    ]


def invert_into(ws, hook):
    n = ws[0].shape[0]

    def body(kb, carry):
        hook(kb)
        o = pl.multiple_of(kb * 128, 128)
        blk = pl.ds(o, 128)
        ps = invert_tiles([[w[pl.ds(o + 8 * i, 8), blk] for i in range(16)] for w in ws])
        for w, p in zip(ws, ps):
            rr = dot(p, w[blk, :])
            c = w[:, blk]
            w[:, blk] = jnp.zeros((n, 128), F32)
            w[blk, :] = rr
            w[blk, blk] = p
            rr2 = w[blk, :]
            w[...] = w[...] - dot(c, rr2)
            w[blk, :] = rr2
        return carry

    lax.fori_loop(0, n // 128, body, 0)


def bits():
    col_bit = lax.axis_index("gx") // (lax.axis_size("gx") // 2)
    row_bit = lax.axis_index("gy") // (lax.axis_size("gy") // 2)
    return col_bit, row_bit


def edges(e):
    col_bit, row_bit = bits()
    starts = (e * (1 - col_bit), 3 * e - e * row_bit, e * col_bit, 2 * e + e * row_bit)
    return [pl.multiple_of(s, e) for s in starts]


def peers():
    gx, gy = lax.axis_index("gx"), lax.axis_index("gy")
    nx, ny = lax.axis_size("gx"), lax.axis_size("gy")
    return (lax.rem(gx + nx // 2, nx), gy), (gx, lax.rem(gy + ny // 2, ny))


def vspec():
    return pl.BlockSpec(memory_space=pltpu.VMEM)


def aspec():
    return pl.BlockSpec(memory_space=pl.ANY)


def shape(*dims, dtype=F32):
    return jax.ShapeDtypeStruct(dims, dtype)


def cost(flops, nbytes):
    return pl.CostEstimate(flops=flops, bytes_accessed=nbytes, transcendentals=0)


CHUNKS = 4
MESH = pl.DeviceIdType.MESH


def group_kernel(
    t_ref, g_ref, f_ref, tu_ref, th_ref, tl_ref,
    blk, lft, mid_cols, gv, gh, gl, f0, csib, h, r, rz, rh, rs, x1, x1z, x2, w1, w1z,
    lsem, fsem, xs, xr, zs, zr,
):
    e = x1.shape[0]
    wid = h.shape[2]
    starts = edges(e)
    inner, mid, side, outer = starts
    px, pz = peers()

    def local(src, dst, sem):
        return pltpu.make_async_copy(src, dst, sem)

    rows = lambda s: pl.ds(s, e)
    loads = [
        local(t_ref.at[rows(inner), rows(inner)], blk.at[0, 0], lsem.at[0]),
        local(t_ref.at[rows(inner), rows(mid)], blk.at[0, 1], lsem.at[1]),
        local(t_ref.at[rows(mid), rows(mid)], blk.at[0, 2], lsem.at[2]),
        local(g_ref, gv, lsem.at[3]),
    ]
    for k in range(4):
        for n, s in enumerate((side, outer)):
            loads.append(
                local(t_ref.at[rows(starts[k]), rows(s)], lft.at[k, :, pl.ds(n * e, e)], lsem.at[4 + 2 * k + n])
            )
    for n, s in enumerate((inner, mid)):
        loads.append(local(t_ref.at[:, rows(s)], mid_cols.at[:, pl.ds(n * e, e)], lsem.at[12 + n]))
    for c in loads:
        c.start()

    barrier = pltpu.get_barrier_semaphore()
    for p in (px, pz):
        pl.semaphore_signal(barrier, inc=1, device_id=p, device_id_type=MESH)
    pl.semaphore_wait(barrier, 2)

    def remote(src, dst, ssem, rsem, n, dev):
        return pltpu.make_async_remote_copy(
            src_ref=src, dst_ref=dst, send_sem=ssem.at[n], recv_sem=rsem.at[n],
            device_id=dev, device_id_type=MESH,
        )

    cols = lambda q: pl.ds(q * wid, wid)
    x_blk = [remote(blk.at[0, k], blk.at[1, k], xs, xr, k, px) for k in range(3)]
    z_blk = [remote(blk.at[0, k], blk.at[2, k], zs, zr, k, pz) for k in range(3)]
    x_fwd = [remote(blk.at[2, k], blk.at[3, k], xs, xr, 3 + k, px) for k in range(3)]
    x_c = [remote(f0.at[0, :, cols(q)], csib.at[q], xs, xr, 6 + q, px) for q in range(CHUNKS)]
    x_r = [remote(rh.at[q], rs.at[q], xs, xr, 6 + CHUNKS + q, px) for q in range(CHUNKS)]
    z_r = [remote(r.at[q], rz.at[q], zs, zr, 3 + q, pz) for q in range(CHUNKS)]

    loads[0].wait()
    x_blk[0].start()
    z_blk[0].start()
    loads[1].wait()
    z_blk[1].start()
    loads[2].wait()
    z_blk[2].start()
    loads[3].wait()
    hi, lo = split(gv[...])
    gh[...] = hi
    gl[...] = lo

    def known(k, q):
        sl = pl.ds(pl.multiple_of(q * wid, wid), wid)
        f0[k, :, sl] = dot3(split(lft[k]), (gh[:, sl], gl[:, sl]))

    def save(k):
        return local(f0.at[k], f_ref.at[rows(starts[k]), :], fsem.at[k])

    loads[4].wait()
    loads[5].wait()
    known(0, 0)
    x_c[0].start()
    lax.fori_loop(1, CHUNKS, lambda q, c: (known(0, q), c)[1], 0)
    for c in loads[6:]:
        c.wait()

    def rest(n, carry):
        known(1 + n // CHUNKS, lax.rem(n, CHUNKS))
        return carry

    lax.fori_loop(0, 3 * CHUNKS, rest, 0)
    for k in range(4):
        save(k).start()

    z_blk[0].wait_recv()
    x_fwd[0].start()
    for q in range(1, CHUNKS):
        x_c[q].start()
    x_blk[1].start()
    x_blk[2].start()
    hi, lo = split(mid_cols[...])
    th_ref[...] = hi
    tl_ref[...] = lo
    x_blk[0].wait_recv()
    x1[...] = blk[0, 0] + blk[1, 0]
    x_fwd[0].wait_recv()
    x1z[...] = blk[2, 0] + blk[3, 0]

    def hook_first(kb):
        @pl.when(kb == 1)
        def _():
            z_blk[1].wait_recv()
            x_fwd[1].start()

    invert_into([x1, x1z], hook_first)
    z_blk[2].wait_recv()
    x_fwd[2].start()

    for q in range(CHUNKS):
        x_c[q].wait_recv()
        h[q] = dot(x1[...], f0[0, :, cols(q)] + csib[q])
        r[q] = f0[1, :, cols(q)] - dot(blk[0, 1], h[q], ((0,), (0,)))
        z_r[q].start()

    x_blk[1].wait_recv()
    w1[:, :e] = dot(x1[...], blk[0, 1])
    w1[:, e:] = dot(x1[...], blk[1, 1])
    x_fwd[1].wait_recv()
    w1z[:, :e] = dot(x1z[...], blk[2, 1])
    w1z[:, e:] = dot(x1z[...], blk[3, 1])
    tn = ((0,), (0,))
    cross = dot(blk[0, 1], w1[:, e:], tn) + dot(blk[2, 1], w1z[:, e:], tn)
    x2[:e, e:] = -cross
    x2[e:, :e] = -cross.T
    own = dot(blk[0, 1], w1[:, :e], tn) + dot(blk[2, 1], w1z[:, :e], tn)
    x2[:e, :e] = blk[0, 2] + blk[2, 2] - own
    sib = dot(blk[1, 1], w1[:, e:], tn) + dot(blk[3, 1], w1z[:, e:], tn)
    x_blk[2].wait_recv()
    x_fwd[2].wait_recv()
    x2[e:, e:] = blk[1, 2] + blk[3, 2] - sib

    def forward(q):
        z_r[q].wait_recv()
        rh[q] = r[q] + rz[q]
        x_r[q].start()

    def hook_second(kb):
        for q in range(CHUNKS - 1):

            @pl.when(kb == q + 1)
            def _():
                forward(q)

    invert_into([x2], hook_second)
    forward(CHUNKS - 1)
    for q in range(CHUNKS):
        x_r[q].wait_recv()
        top = -dot(x2[...], jnp.concatenate([rh[q], rs[q]], 0))
        tu_ref[e:, cols(q)] = top[:e]
        tu_ref[:e, cols(q)] = -(h[q] + dot(w1[...], top))

    for c in x_blk + z_blk + x_fwd + x_c + x_r + z_r:
        c.wait_send()
    for k in range(4):
        save(k).wait()


def last_kernel(th_ref, tl_ref, g_ref, f_ref, tu_ref, p_ref, q_ref):
    e = g_ref.shape[0] // 2
    inner, mid, side, outer = edges(e)
    p_ref[pl.ds(inner, e), :] = tu_ref[:e, :]
    p_ref[pl.ds(mid, e), :] = tu_ref[e:, :]
    p_ref[pl.ds(side, e), :] = g_ref[:e, :]
    p_ref[pl.ds(outer, e), :] = g_ref[e:, :]
    q_ref[...] = f_ref[...] + dot3((th_ref[...], tl_ref[...]), split(tu_ref[...]))


def per_device(leaf_maps, edge_data):
    t = leaf_maps[0, 0]
    g = edge_data[0, 0]
    full = t.shape[0]
    cols = g.shape[1]
    e = full // 4
    wid = cols // CHUNKS
    chunk = pltpu.VMEM((CHUNKS, e, wid), F32)
    dma = pltpu.SemaphoreType.DMA
    nx, nz = 6 + 2 * CHUNKS, 3 + CHUNKS

    f0, tu, th, tl = pl.pallas_call(
        group_kernel,
        out_shape=(
            shape(full, cols), shape(2 * e, cols), shape(full, 2 * e, dtype=BF), shape(full, 2 * e, dtype=BF),
        ),
        in_specs=[aspec(), aspec()],
        out_specs=(aspec(), vspec(), vspec(), vspec()),
        scratch_shapes=[
            pltpu.VMEM((4, 3, e, e), F32),
            pltpu.VMEM((4, e, 2 * e), F32),
            pltpu.VMEM((full, 2 * e), F32),
            pltpu.VMEM((2 * e, cols), F32),
            pltpu.VMEM((2 * e, cols), BF),
            pltpu.VMEM((2 * e, cols), BF),
            pltpu.VMEM((4, e, cols), F32),
            chunk, chunk, chunk, chunk, chunk, chunk,
            pltpu.VMEM((e, e), F32),
            pltpu.VMEM((e, e), F32),
            pltpu.VMEM((2 * e, 2 * e), F32),
            pltpu.VMEM((e, 2 * e), F32),
            pltpu.VMEM((e, 2 * e), F32),
            dma((14,)), dma((4,)), dma((nx,)), dma((nx,)), dma((nz,)), dma((nz,)),
        ],
        compiler_params=pltpu.CompilerParams(
            collective_id=0, has_side_effects=True, vmem_limit_bytes=56 * 2**20
        ),
        cost_estimate=cost(20 * 10**9, 2**24),
        name="group",
    )(t, g)
    pot, flux = pl.pallas_call(
        last_kernel,
        out_shape=(shape(full, cols), shape(full, cols)),
        grid=(CHUNKS,),
        in_specs=[
            pl.BlockSpec((full, 2 * e), lambda j: (0, 0)),
            pl.BlockSpec((full, 2 * e), lambda j: (0, 0)),
            pl.BlockSpec((2 * e, wid), lambda j: (0, j)),
            pl.BlockSpec((full, wid), lambda j: (0, j)),
            pl.BlockSpec((2 * e, wid), lambda j: (0, j)),
        ],
        out_specs=(
            pl.BlockSpec((full, wid), lambda j: (0, j)),
            pl.BlockSpec((full, wid), lambda j: (0, j)),
        ),
        cost_estimate=cost(6 * full * 2 * e * cols, 2**24),
        name="last",
    )(th, tl, g, f0, tu)
    return (pot[None, None], flux[None, None])


def solution(mesh):
    in_specs = (P("gx", "gy", None, None), P("gx", "gy", None, None))
    out_specs = (P("gx", "gy", None, None), P("gx", "gy", None, None))
    return jax.shard_map(
        per_device, mesh=mesh, in_specs=in_specs, out_specs=out_specs, check_vma=False
    )
```

profile of v0, /device:TPU:40, one launch (start us, length us, event | category | flops | bytes accessed | tf_op | source)
XLA Modules:
  0.0 119.5 jit_solution(18118777780826104594)
XLA Ops:
  0.6 108.9 %group.1 = (f32[1024,1024]{1,0:T(8,128)}, f32[512,1024]{1,0:T(8,128)}, bf16[1024,512]{1,0:T(8,128)(2,1)}, bf16[1024,512]{1,0:T(8,128)(2,1)}) custom-call(f32[1024,1024]{1,0:T(8,128)} %bitcast.4, f32[512,1024]{1,0:T(8,128)} %bitcast.5), custom_call_target="tpu_custom_call" | custom-call | flops 20000000000 | bytes 16777216 | tf_op jit(solution)/shard_map/group/pallas_call | solution.py:329
  109.6 9.9 %last.1 = (f32[1024,1024]{1,0:T(8,128)}, f32[1024,1024]{1,0:T(8,128)}) custom-call(bf16[1024,512]{1,0:T(8,128)(2,1)} %get-tuple-element.8.th_ref, bf16[1024,512]{1,0:T(8,128)(2,1)} %get-tuple-element.9.tl_ref, f32[512,1024]{1,0:T(8,128)} %bitcast.6, f32[1024,1024]{1,0:T(8,128)} %get-tuple-element.10.f_ref, f32[512,1024]{1,0:T(8,128)} %get-tuple-element.11.tu_ref), custom_call_target="tpu_custom_call" | custom-call | flops 3221225472 | bytes 16777216 | tf_op jit(solution)/shard_map/last/pallas_call | solution.py:358
where the time goes:
time: 120 us
  Pallas kernels  119 us (99%)
    pallas_call x1, Pallas kernels, per_device(): pl.pallas_call(group_kernel, out_shape=(shape(full, cols), shape(2 * e, c...  109 us
    pallas_call x1, Pallas kernels, per_device(): pl.pallas_call(last_kernel, out_shape=(shape(full, cols), shape(full, col...  9.94 us

commit v1 on v0

--- a/solution.py
+++ b/solution.py
@@ -144,24 +144,28 @@
 
 
 CHUNKS = 4
+PIECES = 8
 MESH = pl.DeviceIdType.MESH
 
 
 def group_kernel(
     t_ref, g_ref, f_ref, tu_ref, th_ref, tl_ref,
-    blk, lft, mid_cols, gv, gh, gl, f0, csib, h, r, rz, rh, rs, x1, x1z, x2, w1, w1z,
+    blk, lft, mid_cols, gv, gh, gl, f0, csib, h, r, rz, rh, rs, x1, x2, w1,
+    mp, mz, mh, ms, x1h, x1l, x2h, x2l, wh, wl, bh, bl,
     lsem, fsem, xs, xr, zs, zr,
 ):
     e = x1.shape[0]
+    half = e // 2
     wid = h.shape[2]
+    pie = r.shape[2]
     starts = edges(e)
     inner, mid, side, outer = starts
     px, pz = peers()
-
-    def local(src, dst, sem):
-        return pltpu.make_async_copy(src, dst, sem)
+    is_left = bits()[0] == 0
+    tn = ((0,), (0,))
 
     rows = lambda s: pl.ds(s, e)
+    local = pltpu.make_async_copy
     loads = [
         local(t_ref.at[rows(inner), rows(inner)], blk.at[0, 0], lsem.at[0]),
         local(t_ref.at[rows(inner), rows(mid)], blk.at[0, 1], lsem.at[1]),
@@ -189,120 +193,142 @@
             device_id=dev, device_id_type=MESH,
         )
 
-    cols = lambda q: pl.ds(q * wid, wid)
-    x_blk = [remote(blk.at[0, k], blk.at[1, k], xs, xr, k, px) for k in range(3)]
-    z_blk = [remote(blk.at[0, k], blk.at[2, k], zs, zr, k, pz) for k in range(3)]
-    x_fwd = [remote(blk.at[2, k], blk.at[3, k], xs, xr, 3 + k, px) for k in range(3)]
-    x_c = [remote(f0.at[0, :, cols(q)], csib.at[q], xs, xr, 6 + q, px) for q in range(CHUNKS)]
-    x_r = [remote(rh.at[q], rs.at[q], xs, xr, 6 + CHUNKS + q, px) for q in range(CHUNKS)]
-    z_r = [remote(r.at[q], rz.at[q], zs, zr, 3 + q, pz) for q in range(CHUNKS)]
+    cols = lambda q: pl.ds(pl.multiple_of(q * wid, wid), wid)
+    x_blk = [remote(blk.at[0, k], blk.at[1, k], xs, xr, k, px) for k in range(2)]
+    x_m = remote(mh, ms, xs, xr, 2, px)
+    z_m = remote(mp, mz, zs, zr, 0, pz)
+    x_c = lambda q: remote(f0.at[0, :, cols(q)], csib.at[q], xs, xr, 3 + q, px)
+    x_r = lambda p: remote(rh.at[p], rs.at[p], xs, xr, 3 + CHUNKS + p, px)
+    z_r = lambda p: remote(r.at[p], rz.at[p], zs, zr, 1 + p, pz)
 
     loads[0].wait()
     x_blk[0].start()
-    z_blk[0].start()
     loads[1].wait()
-    z_blk[1].start()
-    loads[2].wait()
-    z_blk[2].start()
+    x_blk[1].start()
     loads[3].wait()
     hi, lo = split(gv[...])
     gh[...] = hi
     gl[...] = lo
 
     def known(k, q):
-        sl = pl.ds(pl.multiple_of(q * wid, wid), wid)
+        sl = cols(q)
         f0[k, :, sl] = dot3(split(lft[k]), (gh[:, sl], gl[:, sl]))
 
-    def save(k):
-        return local(f0.at[k], f_ref.at[rows(starts[k]), :], fsem.at[k])
-
-    loads[4].wait()
-    loads[5].wait()
-    known(0, 0)
-    x_c[0].start()
-    lax.fori_loop(1, CHUNKS, lambda q, c: (known(0, q), c)[1], 0)
-    for c in loads[6:]:
+    def loop(n, body):
+        def step(i, carry):
+            body(i)
+            return carry
+
+        lax.fori_loop(0, n, step, 0)
+
+    for c in loads[4:8]:
         c.wait()
-
-    def rest(n, carry):
-        known(1 + n // CHUNKS, lax.rem(n, CHUNKS))
-        return carry
-
-    lax.fori_loop(0, 3 * CHUNKS, rest, 0)
-    for k in range(4):
-        save(k).start()
-
-    z_blk[0].wait_recv()
-    x_fwd[0].start()
-    for q in range(1, CHUNKS):
-        x_c[q].start()
-    x_blk[1].start()
-    x_blk[2].start()
-    hi, lo = split(mid_cols[...])
-    th_ref[...] = hi
-    tl_ref[...] = lo
+    loop(CHUNKS, lambda q: known(0, q))
+    loop(CHUNKS, lambda q: x_c(q).start())
+    loop(CHUNKS, lambda q: known(1, q))
     x_blk[0].wait_recv()
     x1[...] = blk[0, 0] + blk[1, 0]
-    x_fwd[0].wait_recv()
-    x1z[...] = blk[2, 0] + blk[3, 0]
-
-    def hook_first(kb):
-        @pl.when(kb == 1)
-        def _():
-            z_blk[1].wait_recv()
-            x_fwd[1].start()
-
-    invert_into([x1, x1z], hook_first)
-    z_blk[2].wait_recv()
-    x_fwd[2].start()
-
-    for q in range(CHUNKS):
-        x_c[q].wait_recv()
-        h[q] = dot(x1[...], f0[0, :, cols(q)] + csib[q])
-        r[q] = f0[1, :, cols(q)] - dot(blk[0, 1], h[q], ((0,), (0,)))
-        z_r[q].start()
-
+    invert_into([x1], lambda kb: None)
     x_blk[1].wait_recv()
+    loads[2].wait()
     w1[:, :e] = dot(x1[...], blk[0, 1])
     w1[:, e:] = dot(x1[...], blk[1, 1])
-    x_fwd[1].wait_recv()
-    w1z[:, :e] = dot(x1z[...], blk[2, 1])
-    w1z[:, e:] = dot(x1z[...], blk[3, 1])
-    tn = ((0,), (0,))
-    cross = dot(blk[0, 1], w1[:, e:], tn) + dot(blk[2, 1], w1z[:, e:], tn)
-    x2[:e, e:] = -cross
-    x2[e:, :e] = -cross.T
-    own = dot(blk[0, 1], w1[:, :e], tn) + dot(blk[2, 1], w1z[:, :e], tn)
-    x2[:e, :e] = blk[0, 2] + blk[2, 2] - own
-    sib = dot(blk[1, 1], w1[:, e:], tn) + dot(blk[3, 1], w1z[:, e:], tn)
-    x_blk[2].wait_recv()
-    x_fwd[2].wait_recv()
-    x2[e:, e:] = blk[1, 2] + blk[3, 2] - sib
-
-    def forward(q):
-        z_r[q].wait_recv()
-        rh[q] = r[q] + rz[q]
-        x_r[q].start()
-
-    def hook_second(kb):
-        for q in range(CHUNKS - 1):
-
-            @pl.when(kb == q + 1)
-            def _():
-                forward(q)
-
-    invert_into([x2], hook_second)
-    forward(CHUNKS - 1)
-    for q in range(CHUNKS):
-        x_r[q].wait_recv()
-        top = -dot(x2[...], jnp.concatenate([rh[q], rs[q]], 0))
+    mp[:e, :] = blk[0, 2] - dot(blk[0, 1], w1[:, :e], tn)
+    part = jnp.where(is_left, blk[0, 1, :, :half], blk[1, 1, :, half:])
+    mp[e:, :] = -dot(part, jnp.where(is_left, w1[:, e:], w1[:, :e]), tn)
+    z_m.start()
+
+    def keep(ref_hi, ref_lo, val):
+        a, b = split(val)
+        ref_hi[...] = a
+        ref_lo[...] = b
+
+    keep(x1h, x1l, x1[...])
+    keep(wh, wl, w1[...])
+    keep(bh, bl, blk[0, 1].T)
+
+    def right(q):
+        x_c(q).wait_recv()
+        hv = dot3((x1h[...], x1l[...]), split(f0[0, :, cols(q)] + csib[q]))
+        h[q] = hv
+        rv = f0[1, :, cols(q)] - dot3((bh[...], bl[...]), split(hv))
+        for n in range(2):
+            r[2 * q + n] = rv[:, n * pie : (n + 1) * pie]
+        for n in range(2):
+            z_r(2 * q + n).start()
+
+    loop(CHUNKS, right)
+
+    for c in loads[8:]:
+        c.wait()
+    loop(2 * CHUNKS, lambda n: known(2 + n // CHUNKS, lax.rem(n, CHUNKS)))
+    save = [local(f0.at[k], f_ref.at[rows(starts[k]), :], fsem.at[k]) for k in range(4)]
+    for c in save:
+        c.start()
+    keep(th_ref, tl_ref, mid_cols[...])
+
+    z_m.wait_recv()
+    mh[...] = mp[...] + mz[...]
+    x_m.start()
+    x_m.wait_recv()
+    x2[:e, :e] = mh[:e, :]
+    x2[e:, e:] = ms[:e, :]
+    upper = jnp.where(is_left, mh[e:, :], ms[e:, :])
+    lower = jnp.where(is_left, ms[e:, :], mh[e:, :])
+    cross = jnp.concatenate([upper, lower], 0)
+    cross_t = cross.T
+    x2[:e, e:] = jnp.where(is_left, cross, cross_t)
+    x2[e:, :e] = jnp.where(is_left, cross_t, cross)
+
+    def forward(p):
+        z_r(p).wait_recv()
+        rh[p] = r[p] + rz[p]
+        x_r(p).start()
+
+    def hook(kb):
+        @pl.when((kb == 1) | (kb == 2))
+        def _():
+            forward(2 * kb - 2)
+            forward(2 * kb - 1)
+
+        @pl.when(kb == 3)
+        def _():
+            forward(4)
+
+    invert_into([x2], hook)
+    keep(x2h, x2l, x2[...])
+
+    def solve(q):
+        @pl.when(q < PIECES - 5)
+        def _():
+            forward(q + 5)
+
+        x_r(2 * q).wait_recv()
+        x_r(2 * q + 1).wait_recv()
+        rhs = jnp.concatenate(
+            [
+                jnp.concatenate([rh[2 * q], rh[2 * q + 1]], 1),
+                jnp.concatenate([rs[2 * q], rs[2 * q + 1]], 1),
+            ],
+            0,
+        )
+        top = -dot3((x2h[...], x2l[...]), split(rhs))
         tu_ref[e:, cols(q)] = top[:e]
-        tu_ref[:e, cols(q)] = -(h[q] + dot(w1[...], top))
-
-    for c in x_blk + z_blk + x_fwd + x_c + x_r + z_r:
+        tu_ref[:e, cols(q)] = -(h[q] + dot3((wh[...], wl[...]), split(top)))
+
+    loop(CHUNKS, solve)
+
+    for c in x_blk + [x_m, z_m]:
         c.wait_send()
-    for k in range(4):
-        save(k).wait()
+    loop(CHUNKS, lambda q: x_c(q).wait_send())
+
+    def sent(p):
+        x_r(p).wait_send()
+        z_r(p).wait_send()
+
+    loop(PIECES, sent)
+    for c in save:
+        c.wait()
 
 
 def last_kernel(th_ref, tl_ref, g_ref, f_ref, tu_ref, p_ref, q_ref):
@@ -323,8 +349,13 @@
     e = full // 4
     wid = cols // CHUNKS
     chunk = pltpu.VMEM((CHUNKS, e, wid), F32)
+    piece = pltpu.VMEM((PIECES, e, cols // PIECES), F32)
+    half_sum = pltpu.VMEM((e + e // 2, e), F32)
+    square = pltpu.VMEM((e, e), BF)
+    square2 = pltpu.VMEM((2 * e, 2 * e), BF)
+    wide = pltpu.VMEM((e, 2 * e), BF)
     dma = pltpu.SemaphoreType.DMA
-    nx, nz = 6 + 2 * CHUNKS, 3 + CHUNKS
+    nx, nz = 3 + CHUNKS + PIECES, 1 + PIECES
 
     f0, tu, th, tl = pl.pallas_call(
         group_kernel,
@@ -334,19 +365,19 @@
         in_specs=[aspec(), aspec()],
         out_specs=(aspec(), vspec(), vspec(), vspec()),
         scratch_shapes=[
-            pltpu.VMEM((4, 3, e, e), F32),
+            pltpu.VMEM((2, 3, e, e), F32),
             pltpu.VMEM((4, e, 2 * e), F32),
             pltpu.VMEM((full, 2 * e), F32),
             pltpu.VMEM((2 * e, cols), F32),
             pltpu.VMEM((2 * e, cols), BF),
             pltpu.VMEM((2 * e, cols), BF),
             pltpu.VMEM((4, e, cols), F32),
-            chunk, chunk, chunk, chunk, chunk, chunk,
-            pltpu.VMEM((e, e), F32),
+            chunk, chunk, piece, piece, piece, piece,
             pltpu.VMEM((e, e), F32),
             pltpu.VMEM((2 * e, 2 * e), F32),
             pltpu.VMEM((e, 2 * e), F32),
-            pltpu.VMEM((e, 2 * e), F32),
+            half_sum, half_sum, half_sum, half_sum,
+            square, square, square2, square2, wide, wide, square, square,
             dma((14,)), dma((4,)), dma((nx,)), dma((nx,)), dma((nz,)), dma((nz,)),
         ],
         compiler_params=pltpu.CompilerParams(

time: 120 us -> 112 us (0.933)
  the two profiles are of different devices: /device:TPU:40 before, /device:TPU:16 now
where the time goes in v1:
time: 112 us
  Pallas kernels  111 us (99%)
    pallas_call x1, Pallas kernels, per_device(): pl.pallas_call(group_kernel, out_shape=(shape(full, cols), shape(2 * e, c...  101 us
    pallas_call x1, Pallas kernels, per_device(): pl.pallas_call(last_kernel, out_shape=(shape(full, cols), shape(full, col...  9.94 us

profile of v1, /device:TPU:16, one launch (start us, length us, event | category | flops | bytes accessed | tf_op | source)
XLA Modules:
  0.0 111.7 jit_solution(717408164109655411)
XLA Ops:
  0.6 101.2 %group.1 = (f32[1024,1024]{1,0:T(8,128)}, f32[512,1024]{1,0:T(8,128)}, bf16[1024,512]{1,0:T(8,128)(2,1)}, bf16[1024,512]{1,0:T(8,128)(2,1)}) custom-call(f32[1024,1024]{1,0:T(8,128)} %bitcast.4, f32[512,1024]{1,0:T(8,128)} %bitcast.5), custom_call_target="tpu_custom_call" | custom-call | flops 20000000000 | bytes 16777216 | tf_op jit(solution)/shard_map/group/pallas_call | solution.py:360
  101.8 9.9 %last.1 = (f32[1024,1024]{1,0:T(8,128)}, f32[1024,1024]{1,0:T(8,128)}) custom-call(bf16[1024,512]{1,0:T(8,128)(2,1)} %get-tuple-element.8.th_ref, bf16[1024,512]{1,0:T(8,128)(2,1)} %get-tuple-element.9.tl_ref, f32[512,1024]{1,0:T(8,128)} %bitcast.6, f32[1024,1024]{1,0:T(8,128)} %get-tuple-element.10.f_ref, f32[512,1024]{1,0:T(8,128)} %get-tuple-element.11.tu_ref), custom_call_target="tpu_custom_call" | custom-call | flops 3221225472 | bytes 16777216 | tf_op jit(solution)/shard_map/last/pallas_call | solution.py:389

commit v2 on v1

--- a/solution.py
+++ b/solution.py
@@ -87,7 +87,7 @@
     ]
 
 
-def invert_into(ws, hook):
+def invert_into(ws, hook, fill):
     n = ws[0].shape[0]
 
     def body(kb, carry):
@@ -95,6 +95,7 @@
         o = pl.multiple_of(kb * 128, 128)
         blk = pl.ds(o, 128)
         ps = invert_tiles([[w[pl.ds(o + 8 * i, 8), blk] for i in range(16)] for w in ws])
+        fill(kb)
         for w, p in zip(ws, ps):
             rr = dot(p, w[blk, :])
             c = w[:, blk]
@@ -151,8 +152,8 @@
 def group_kernel(
     t_ref, g_ref, f_ref, tu_ref, th_ref, tl_ref,
     blk, lft, mid_cols, gv, gh, gl, f0, csib, h, r, rz, rh, rs, x1, x2, w1,
-    mp, mz, mh, ms, x1h, x1l, x2h, x2l, wh, wl, bh, bl,
-    lsem, fsem, xs, xr, zs, zr,
+    mp, mz, mh, ms, x1h, x1l, x2h, x2l, wh, wl, bh, bl, tuv, thv, tlv,
+    lsem, fsem, osem, xs, xr, zs, zr,
 ):
     e = x1.shape[0]
     half = e // 2
@@ -194,21 +195,33 @@
         )
 
     cols = lambda q: pl.ds(pl.multiple_of(q * wid, wid), wid)
-    x_blk = [remote(blk.at[0, k], blk.at[1, k], xs, xr, k, px) for k in range(2)]
-    x_m = remote(mh, ms, xs, xr, 2, px)
+    lo, hi = slice(0, half), slice(half, e)
+    x_in = [
+        remote(blk.at[0, 0, i, j], blk.at[1, 0, i, j], xs, xr, n, px)
+        for n, (i, j) in enumerate(
+            (pl.ds(p * half, half), pl.ds(q * half, half)) for p, q in ((0, 0), (1, 0), (1, 1))
+        )
+    ]
+    x_b = remote(blk.at[0, 1], blk.at[1, 1], xs, xr, 3, px)
+    x_m = remote(mh, ms, xs, xr, 4, px)
     z_m = remote(mp, mz, zs, zr, 0, pz)
-    x_c = lambda q: remote(f0.at[0, :, cols(q)], csib.at[q], xs, xr, 3 + q, px)
-    x_r = lambda p: remote(rh.at[p], rs.at[p], xs, xr, 3 + CHUNKS + p, px)
+    x_c = lambda q: remote(f0.at[0, :, cols(q)], csib.at[q], xs, xr, 5 + q, px)
+    x_r = lambda p: remote(rh.at[p], rs.at[p], xs, xr, 5 + CHUNKS + p, px)
     z_r = lambda p: remote(r.at[p], rz.at[p], zs, zr, 1 + p, pz)
 
     loads[0].wait()
-    x_blk[0].start()
+    for c in x_in:
+        c.start()
     loads[1].wait()
-    x_blk[1].start()
+    x_b.start()
+
+    def keep(ref_hi, ref_lo, val):
+        a, b = split(val)
+        ref_hi[...] = a
+        ref_lo[...] = b
+
     loads[3].wait()
-    hi, lo = split(gv[...])
-    gh[...] = hi
-    gl[...] = lo
+    keep(gh, gl, gv[...])
 
     def known(k, q):
         sl = cols(q)
@@ -221,33 +234,68 @@
 
         lax.fori_loop(0, n, step, 0)
 
-    for c in loads[4:8]:
+    for c in loads[4:6]:
         c.wait()
     loop(CHUNKS, lambda q: known(0, q))
     loop(CHUNKS, lambda q: x_c(q).start())
-    loop(CHUNKS, lambda q: known(1, q))
-    x_blk[0].wait_recv()
-    x1[...] = blk[0, 0] + blk[1, 0]
-    invert_into([x1], lambda kb: None)
-    x_blk[1].wait_recv()
+
+    x_in[0].wait_recv()
+    x1[lo, lo] = blk[0, 0, lo, lo] + blk[1, 0, lo, lo]
+
+    def fill_first(kb):
+        @pl.when(kb == 0)
+        def _():
+            x_in[1].wait_recv()
+            x_in[2].wait_recv()
+            below = blk[0, 0, hi, lo] + blk[1, 0, hi, lo]
+            x1[hi, lo] = below
+            x1[lo, hi] = below.T
+            x1[hi, hi] = blk[0, 0, hi, hi] + blk[1, 0, hi, hi]
+
+    invert_into([x1], lambda kb: None, fill_first)
+    x_b.wait_recv()
     loads[2].wait()
     w1[:, :e] = dot(x1[...], blk[0, 1])
     w1[:, e:] = dot(x1[...], blk[1, 1])
-    mp[:e, :] = blk[0, 2] - dot(blk[0, 1], w1[:, :e], tn)
-    part = jnp.where(is_left, blk[0, 1, :, :half], blk[1, 1, :, half:])
-    mp[e:, :] = -dot(part, jnp.where(is_left, w1[:, e:], w1[:, :e]), tn)
+    strip = blk[0, 2, :, lo] - dot(blk[0, 1], w1[:, lo], tn)
+    mp[0] = strip[lo]
+    mp[1] = strip[hi]
+    mp[2] = blk[0, 2, hi, hi] - dot(blk[0, 1, :, hi], w1[:, hi], tn)
+    part = jnp.where(is_left, blk[0, 1, :, lo], blk[1, 1, :, hi])
+    cross = -dot(part, jnp.where(is_left, w1[:, e:], w1[:, :e]), tn)
+    mp[3] = cross[:, lo]
+    mp[4] = cross[:, hi]
     z_m.start()
 
-    def keep(ref_hi, ref_lo, val):
-        a, b = split(val)
-        ref_hi[...] = a
-        ref_lo[...] = b
-
     keep(x1h, x1l, x1[...])
-    keep(wh, wl, w1[...])
     keep(bh, bl, blk[0, 1].T)
+    for c in loads[6:8]:
+        c.wait()
+    loop(CHUNKS, lambda q: known(1, q))
+
+    last = CHUNKS - 1
+    parts = [
+        local(thv, th_ref, osem.at[0]),
+        local(tlv, tl_ref, osem.at[1]),
+    ]
+    out_t = lambda q: local(tuv.at[:, cols(q)], tu_ref.at[:, cols(q)], osem.at[2 + q])
+
+    def out_f(k, q):
+        return local(f0.at[k, :, cols(q)], f_ref.at[rows(starts[k]), cols(q)], fsem.at[k, q])
 
     def right(q):
+        @pl.when(q == 2)
+        def _():
+            for c in loads[8:]:
+                c.wait()
+            loop(2 * CHUNKS, lambda n: known(2 + n // CHUNKS, lax.rem(n, CHUNKS)))
+            for k in range(4):
+                out_f(k, last).start()
+            keep(thv, tlv, mid_cols[...])
+            for c in parts:
+                c.start()
+            keep(wh, wl, w1[...])
+
         x_c(q).wait_recv()
         hv = dot3((x1h[...], x1l[...]), split(f0[0, :, cols(q)] + csib[q]))
         h[q] = hv
@@ -259,26 +307,10 @@
 
     loop(CHUNKS, right)
 
-    for c in loads[8:]:
-        c.wait()
-    loop(2 * CHUNKS, lambda n: known(2 + n // CHUNKS, lax.rem(n, CHUNKS)))
-    save = [local(f0.at[k], f_ref.at[rows(starts[k]), :], fsem.at[k]) for k in range(4)]
-    for c in save:
-        c.start()
-    keep(th_ref, tl_ref, mid_cols[...])
-
     z_m.wait_recv()
     mh[...] = mp[...] + mz[...]
     x_m.start()
-    x_m.wait_recv()
-    x2[:e, :e] = mh[:e, :]
-    x2[e:, e:] = ms[:e, :]
-    upper = jnp.where(is_left, mh[e:, :], ms[e:, :])
-    lower = jnp.where(is_left, ms[e:, :], mh[e:, :])
-    cross = jnp.concatenate([upper, lower], 0)
-    cross_t = cross.T
-    x2[:e, e:] = jnp.where(is_left, cross, cross_t)
-    x2[e:, :e] = jnp.where(is_left, cross_t, cross)
+    x2[lo, lo] = mh[0]
 
     def forward(p):
         z_r(p).wait_recv()
@@ -286,23 +318,47 @@
         x_r(p).start()
 
     def hook(kb):
-        @pl.when((kb == 1) | (kb == 2))
-        def _():
-            forward(2 * kb - 2)
-            forward(2 * kb - 1)
+        @pl.when(kb == 1)
+        def _():
+            forward(0)
+
+        @pl.when(kb == 2)
+        def _():
+            forward(1)
+            forward(2)
 
         @pl.when(kb == 3)
         def _():
-            forward(4)
-
-    invert_into([x2], hook)
+            forward(3)
+
+    def fill_second(kb):
+        @pl.when(kb == 0)
+        def _():
+            x2[hi, lo] = mh[1]
+            x2[lo, hi] = mh[1].T
+            x2[hi, hi] = mh[2]
+            x_m.wait_recv()
+            low, high = slice(e, e + half), slice(e + half, 2 * e)
+            x2[low, low] = ms[0]
+            x2[high, low] = ms[1]
+            x2[low, high] = ms[1].T
+            x2[high, high] = ms[2]
+            mine = jnp.concatenate([mh[3], mh[4]], 1)
+            other = jnp.concatenate([ms[3], ms[4]], 1)
+            full = jnp.concatenate(
+                [jnp.where(is_left, mine, other), jnp.where(is_left, other, mine)], 0
+            )
+            full_t = full.T
+            x2[:e, e:] = jnp.where(is_left, full, full_t)
+            x2[e:, :e] = jnp.where(is_left, full_t, full)
+
+    invert_into([x2], hook, fill_second)
+    loop(CHUNKS, lambda q: x_c(q).wait_send())
+    forward(4)
+    forward(5)
     keep(x2h, x2l, x2[...])
 
     def solve(q):
-        @pl.when(q < PIECES - 5)
-        def _():
-            forward(q + 5)
-
         x_r(2 * q).wait_recv()
         x_r(2 * q + 1).wait_recv()
         rhs = jnp.concatenate(
@@ -313,22 +369,42 @@
             0,
         )
         top = -dot3((x2h[...], x2l[...]), split(rhs))
-        tu_ref[e:, cols(q)] = top[:e]
-        tu_ref[:e, cols(q)] = -(h[q] + dot3((wh[...], wl[...]), split(top)))
+        tuv[e:, cols(q)] = top[:e]
+        tuv[:e, cols(q)] = -(h[q] + dot3((wh[...], wl[...]), split(top)))
+        out_t(q).start()
+
+        @pl.when(q < last)
+        def _():
+            both = split(tuv[:, cols(q)])
+            for k in range(4):
+                left = (thv[rows(starts[k]), :], tlv[rows(starts[k]), :])
+                f0[k, :, cols(q)] = f0[k, :, cols(q)] + dot3(left, both)
+            for k in range(4):
+                out_f(k, q).start()
+
+        @pl.when(q < 2)
+        def _():
+            forward(6 + q)
 
     loop(CHUNKS, solve)
 
-    for c in x_blk + [x_m, z_m]:
+    for c in x_in + [x_b, x_m, z_m]:
         c.wait_send()
-    loop(CHUNKS, lambda q: x_c(q).wait_send())
 
     def sent(p):
         x_r(p).wait_send()
         z_r(p).wait_send()
 
     loop(PIECES, sent)
-    for c in save:
+    for c in parts:
         c.wait()
+
+    def written(q):
+        out_t(q).wait()
+        for k in range(4):
+            out_f(k, q).wait()
+
+    loop(CHUNKS, written)
 
 
 def last_kernel(th_ref, tl_ref, g_ref, f_ref, tu_ref, p_ref, q_ref):
@@ -338,7 +414,15 @@
     p_ref[pl.ds(mid, e), :] = tu_ref[e:, :]
     p_ref[pl.ds(side, e), :] = g_ref[:e, :]
     p_ref[pl.ds(outer, e), :] = g_ref[e:, :]
-    q_ref[...] = f_ref[...] + dot3((th_ref[...], tl_ref[...]), split(tu_ref[...]))
+    heavy = pl.program_id(0) == 0
+
+    @pl.when(heavy)
+    def _():
+        q_ref[...] = f_ref[...] + dot3((th_ref[...], tl_ref[...]), split(tu_ref[...]))
+
+    @pl.when(jnp.logical_not(heavy))
+    def _():
+        q_ref[...] = f_ref[...]
 
 
 def per_device(leaf_maps, edge_data):
@@ -350,12 +434,12 @@
     wid = cols // CHUNKS
     chunk = pltpu.VMEM((CHUNKS, e, wid), F32)
     piece = pltpu.VMEM((PIECES, e, cols // PIECES), F32)
-    half_sum = pltpu.VMEM((e + e // 2, e), F32)
+    half_sum = pltpu.VMEM((5, e // 2, e // 2), F32)
     square = pltpu.VMEM((e, e), BF)
     square2 = pltpu.VMEM((2 * e, 2 * e), BF)
     wide = pltpu.VMEM((e, 2 * e), BF)
     dma = pltpu.SemaphoreType.DMA
-    nx, nz = 3 + CHUNKS + PIECES, 1 + PIECES
+    nx, nz = 5 + CHUNKS + PIECES, 1 + PIECES
 
     f0, tu, th, tl = pl.pallas_call(
         group_kernel,
@@ -363,7 +447,7 @@
             shape(full, cols), shape(2 * e, cols), shape(full, 2 * e, dtype=BF), shape(full, 2 * e, dtype=BF),
         ),
         in_specs=[aspec(), aspec()],
-        out_specs=(aspec(), vspec(), vspec(), vspec()),
+        out_specs=(aspec(),) * 4,
         scratch_shapes=[
             pltpu.VMEM((2, 3, e, e), F32),
             pltpu.VMEM((4, e, 2 * e), F32),
@@ -378,7 +462,10 @@
             pltpu.VMEM((e, 2 * e), F32),
             half_sum, half_sum, half_sum, half_sum,
             square, square, square2, square2, wide, wide, square, square,
-            dma((14,)), dma((4,)), dma((nx,)), dma((nx,)), dma((nz,)), dma((nz,)),
+            pltpu.VMEM((2 * e, cols), F32),
+            pltpu.VMEM((full, 2 * e), BF),
+            pltpu.VMEM((full, 2 * e), BF),
+            dma((14,)), dma((4, CHUNKS)), dma((2 + CHUNKS,)), dma((nx,)), dma((nx,)), dma((nz,)), dma((nz,)),
         ],
         compiler_params=pltpu.CompilerParams(
             collective_id=0, has_side_effects=True, vmem_limit_bytes=56 * 2**20
@@ -393,13 +480,13 @@
         in_specs=[
             pl.BlockSpec((full, 2 * e), lambda j: (0, 0)),
             pl.BlockSpec((full, 2 * e), lambda j: (0, 0)),
-            pl.BlockSpec((2 * e, wid), lambda j: (0, j)),
-            pl.BlockSpec((full, wid), lambda j: (0, j)),
-            pl.BlockSpec((2 * e, wid), lambda j: (0, j)),
+            pl.BlockSpec((2 * e, wid), lambda j: (0, CHUNKS - 1 - j)),
+            pl.BlockSpec((full, wid), lambda j: (0, CHUNKS - 1 - j)),
+            pl.BlockSpec((2 * e, wid), lambda j: (0, CHUNKS - 1 - j)),
         ],
         out_specs=(
-            pl.BlockSpec((full, wid), lambda j: (0, j)),
-            pl.BlockSpec((full, wid), lambda j: (0, j)),
+            pl.BlockSpec((full, wid), lambda j: (0, CHUNKS - 1 - j)),
+            pl.BlockSpec((full, wid), lambda j: (0, CHUNKS - 1 - j)),
         ),
         cost_estimate=cost(6 * full * 2 * e * cols, 2**24),
         name="last",

time: 112 us -> 103 us (0.920)
  Pallas kernels: 111 us -> 103 us
    pallas_call x1, Pallas kernels: 101 us -> 93.9 us  [per_device(): pl.pallas_call(group_kernel, out_shape=(shape(full, cols), shape(2 * e, c...]
where the time goes in v2:
time: 103 us
  Pallas kernels  103 us (100%)
    pallas_call x1, Pallas kernels, per_device(): pl.pallas_call(group_kernel, out_shape=(shape(full, cols), shape(2 * e, c...  93.9 us
    pallas_call x1, Pallas kernels, per_device(): pl.pallas_call(last_kernel, out_shape=(shape(full, cols), shape(full, col...  8.85 us

profile of v2, /device:TPU:16, one launch (start us, length us, event | category | flops | bytes accessed | tf_op | source)
XLA Modules:
  0.0 103.3 jit_solution(696810197362790609)
XLA Ops:
  0.6 93.9 %group.1 = (f32[1024,1024]{1,0:T(8,128)}, f32[512,1024]{1,0:T(8,128)}, bf16[1024,512]{1,0:T(8,128)(2,1)}, bf16[1024,512]{1,0:T(8,128)(2,1)}) custom-call(f32[1024,1024]{1,0:T(8,128)} %bitcast.4, f32[512,1024]{1,0:T(8,128)} %bitcast.5), custom_call_target="tpu_custom_call" | custom-call | flops 20000000000 | bytes 16777216 | tf_op jit(solution)/shard_map/group/pallas_call | solution.py:444
  94.5 8.9 %last.1 = (f32[1024,1024]{1,0:T(8,128)}, f32[1024,1024]{1,0:T(8,128)}) custom-call(bf16[1024,512]{1,0:T(8,128)(2,1)} %get-tuple-element.8.th_ref, bf16[1024,512]{1,0:T(8,128)(2,1)} %get-tuple-element.9.tl_ref, f32[512,1024]{1,0:T(8,128)} %bitcast.6, f32[1024,1024]{1,0:T(8,128)} %get-tuple-element.10.f_ref, f32[512,1024]{1,0:T(8,128)} %get-tuple-element.11.tu_ref), custom_call_target="tpu_custom_call" | custom-call | flops 3221225472 | bytes 16777216 | tf_op jit(solution)/shard_map/last/pallas_call | solution.py:476

commit v3 on v2

--- a/solution.py
+++ b/solution.py
@@ -136,6 +136,10 @@
     return pl.BlockSpec(memory_space=pl.ANY)
 
 
+def hspec():
+    return pl.BlockSpec(memory_space=pltpu.HBM)
+
+
 def shape(*dims, dtype=F32):
     return jax.ShapeDtypeStruct(dims, dtype)
 
@@ -204,7 +208,10 @@
     ]
     x_b = remote(blk.at[0, 1], blk.at[1, 1], xs, xr, 3, px)
     x_m = remote(mh, ms, xs, xr, 4, px)
-    z_m = remote(mp, mz, zs, zr, 0, pz)
+    z_m = [
+        remote(mp.at[pl.ds(0, 3)], mz.at[pl.ds(0, 3)], zs, zr, 0, pz),
+        remote(mp.at[pl.ds(3, 2)], mz.at[pl.ds(3, 2)], zs, zr, 1 + PIECES, pz),
+    ]
     x_c = lambda q: remote(f0.at[0, :, cols(q)], csib.at[q], xs, xr, 5 + q, px)
     x_r = lambda p: remote(rh.at[p], rs.at[p], xs, xr, 5 + CHUNKS + p, px)
     z_r = lambda p: remote(r.at[p], rz.at[p], zs, zr, 1 + p, pz)
@@ -253,19 +260,20 @@
             x1[hi, hi] = blk[0, 0, hi, hi] + blk[1, 0, hi, hi]
 
     invert_into([x1], lambda kb: None, fill_first)
-    x_b.wait_recv()
     loads[2].wait()
     w1[:, :e] = dot(x1[...], blk[0, 1])
-    w1[:, e:] = dot(x1[...], blk[1, 1])
     strip = blk[0, 2, :, lo] - dot(blk[0, 1], w1[:, lo], tn)
     mp[0] = strip[lo]
     mp[1] = strip[hi]
     mp[2] = blk[0, 2, hi, hi] - dot(blk[0, 1, :, hi], w1[:, hi], tn)
+    z_m[0].start()
+    x_b.wait_recv()
+    w1[:, e:] = dot(x1[...], blk[1, 1])
     part = jnp.where(is_left, blk[0, 1, :, lo], blk[1, 1, :, hi])
     cross = -dot(part, jnp.where(is_left, w1[:, e:], w1[:, :e]), tn)
     mp[3] = cross[:, lo]
     mp[4] = cross[:, hi]
-    z_m.start()
+    z_m[1].start()
 
     keep(x1h, x1l, x1[...])
     keep(bh, bl, blk[0, 1].T)
@@ -307,7 +315,8 @@
 
     loop(CHUNKS, right)
 
-    z_m.wait_recv()
+    z_m[0].wait_recv()
+    z_m[1].wait_recv()
     mh[...] = mp[...] + mz[...]
     x_m.start()
     x2[lo, lo] = mh[0]
@@ -388,7 +397,7 @@
 
     loop(CHUNKS, solve)
 
-    for c in x_in + [x_b, x_m, z_m]:
+    for c in x_in + z_m + [x_b, x_m]:
         c.wait_send()
 
     def sent(p):
@@ -407,27 +416,50 @@
     loop(CHUNKS, written)
 
 
-def last_kernel(th_ref, tl_ref, g_ref, f_ref, tu_ref, p_ref, q_ref):
+def last_kernel(th_ref, tl_ref, g_ref, f_ref, tu_ref, p_ref, q_ref, thv, tlv, gv, fv, tuv, isem, osem):
     e = g_ref.shape[0] // 2
+    cols = g_ref.shape[1]
+    done = cols - cols // CHUNKS
     inner, mid, side, outer = edges(e)
-    p_ref[pl.ds(inner, e), :] = tu_ref[:e, :]
-    p_ref[pl.ds(mid, e), :] = tu_ref[e:, :]
-    p_ref[pl.ds(side, e), :] = g_ref[:e, :]
-    p_ref[pl.ds(outer, e), :] = g_ref[e:, :]
-    heavy = pl.program_id(0) == 0
-
-    @pl.when(heavy)
-    def _():
-        q_ref[...] = f_ref[...] + dot3((th_ref[...], tl_ref[...]), split(tu_ref[...]))
-
-    @pl.when(jnp.logical_not(heavy))
-    def _():
-        q_ref[...] = f_ref[...]
+    copy = pltpu.make_async_copy
+    block = lambda i: pl.ds(i * e, e)
+    ready, late = pl.ds(0, done), pl.ds(done, cols - done)
+    loads = [
+        copy(g_ref, gv, isem.at[0]),
+        copy(tu_ref.at[:, late], tuv, isem.at[1]),
+        copy(th_ref, thv, isem.at[2]),
+        copy(tl_ref, tlv, isem.at[3]),
+    ]
+    loads += [copy(f_ref.at[block(i), late], fv.at[i], isem.at[4 + i]) for i in range(4)]
+    stores = [
+        copy(src.at[block(n)], p_ref.at[pl.ds(s, e), :], osem.at[i])
+        for i, (src, n, s) in enumerate(
+            ((gv, 0, side), (gv, 1, outer), (tu_ref, 0, inner), (tu_ref, 1, mid))
+        )
+    ]
+    stores += [
+        copy(f_ref.at[block(i), ready], q_ref.at[block(i), ready], osem.at[4 + i]) for i in range(4)
+    ]
+    final = [copy(fv.at[i], q_ref.at[block(i), late], osem.at[8 + i]) for i in range(4)]
+    for c in loads + stores[2:]:
+        c.start()
+    loads[0].wait()
+    stores[0].start()
+    stores[1].start()
+    for c in loads[1:4]:
+        c.wait()
+    both = split(tuv[...])
+    for i in range(4):
+        loads[4 + i].wait()
+        fv[i] = fv[i] + dot3((thv[block(i), :], tlv[block(i), :]), both)
+        final[i].start()
+    for c in stores + final:
+        c.wait()
 
 
 def per_device(leaf_maps, edge_data):
-    t = leaf_maps[0, 0]
-    g = edge_data[0, 0]
+    t = pltpu.with_memory_space_constraint(leaf_maps[0, 0], pltpu.HBM)
+    g = pltpu.with_memory_space_constraint(edge_data[0, 0], pltpu.HBM)
     full = t.shape[0]
     cols = g.shape[1]
     e = full // 4
@@ -439,14 +471,14 @@
     square2 = pltpu.VMEM((2 * e, 2 * e), BF)
     wide = pltpu.VMEM((e, 2 * e), BF)
     dma = pltpu.SemaphoreType.DMA
-    nx, nz = 5 + CHUNKS + PIECES, 1 + PIECES
+    nx, nz = 5 + CHUNKS + PIECES, 2 + PIECES
 
     f0, tu, th, tl = pl.pallas_call(
         group_kernel,
         out_shape=(
             shape(full, cols), shape(2 * e, cols), shape(full, 2 * e, dtype=BF), shape(full, 2 * e, dtype=BF),
         ),
-        in_specs=[aspec(), aspec()],
+        in_specs=[hspec(), hspec()],
         out_specs=(aspec(),) * 4,
         scratch_shapes=[
             pltpu.VMEM((2, 3, e, e), F32),
@@ -468,7 +500,7 @@
             dma((14,)), dma((4, CHUNKS)), dma((2 + CHUNKS,)), dma((nx,)), dma((nx,)), dma((nz,)), dma((nz,)),
         ],
         compiler_params=pltpu.CompilerParams(
-            collective_id=0, has_side_effects=True, vmem_limit_bytes=56 * 2**20
+            collective_id=0, has_side_effects=True, vmem_limit_bytes=32 * 2**20
         ),
         cost_estimate=cost(20 * 10**9, 2**24),
         name="group",
@@ -476,18 +508,17 @@
     pot, flux = pl.pallas_call(
         last_kernel,
         out_shape=(shape(full, cols), shape(full, cols)),
-        grid=(CHUNKS,),
-        in_specs=[
-            pl.BlockSpec((full, 2 * e), lambda j: (0, 0)),
-            pl.BlockSpec((full, 2 * e), lambda j: (0, 0)),
-            pl.BlockSpec((2 * e, wid), lambda j: (0, CHUNKS - 1 - j)),
-            pl.BlockSpec((full, wid), lambda j: (0, CHUNKS - 1 - j)),
-            pl.BlockSpec((2 * e, wid), lambda j: (0, CHUNKS - 1 - j)),
+        in_specs=[aspec(), aspec(), hspec(), aspec(), aspec()],
+        out_specs=(aspec(), aspec()),
+        scratch_shapes=[
+            pltpu.VMEM((full, 2 * e), BF),
+            pltpu.VMEM((full, 2 * e), BF),
+            pltpu.VMEM((2 * e, cols), F32),
+            pltpu.VMEM((4, e, wid), F32),
+            pltpu.VMEM((2 * e, wid), F32),
+            dma((8,)), dma((12,)),
         ],
-        out_specs=(
-            pl.BlockSpec((full, wid), lambda j: (0, CHUNKS - 1 - j)),
-            pl.BlockSpec((full, wid), lambda j: (0, CHUNKS - 1 - j)),
-        ),
+        compiler_params=pltpu.CompilerParams(vmem_limit_bytes=12 * 2**20),
         cost_estimate=cost(6 * full * 2 * e * cols, 2**24),
         name="last",
     )(th, tl, g, f0, tu)

time: 103 us -> 99.8 us (0.969)
  Pallas kernels: 103 us -> 98.9 us
    pallas_call x1, Pallas kernels: 8.85 us -> 5.52 us  [per_device(): pl.pallas_call(last_kernel, out_shape=(shape(full, cols), shape(full, col...]
where the time goes in v3:
time: 99.8 us; the launch traced here: 99.7 us
  Pallas kernels  98.9 us (99%)
    pallas_call x1, Pallas kernels, per_device(): pl.pallas_call(group_kernel, out_shape=(shape(full, cols), shape(2 * e, c...  93.4 us
    pallas_call x1, Pallas kernels, per_device(): pl.pallas_call(last_kernel, out_shape=(shape(full, cols), shape(full, col...  5.52 us

profile of v3, /device:TPU:16, one launch (start us, length us, event | category | flops | bytes accessed | tf_op | source)
XLA Modules:
  0.0 99.7 jit_solution(7927742106261702613)
XLA Ops:
  0.6 93.4 %group.1 = (f32[1024,1024]{1,0:T(8,128)S(1)}, f32[512,1024]{1,0:T(8,128)S(1)}, bf16[1024,512]{1,0:T(8,128)(2,1)S(1)}, bf16[1024,512]{1,0:T(8,128)(2,1)S(1)}) custom-call(f32[1024,1024]{1,0:T(8,128)} %bitcast.4, f32[512,1024]{1,0:T(8,128)} %bitcast.5), custom_call_target="tpu_custom_call" | custom-call | flops 20000000000 | bytes 16777216 | tf_op jit(solution)/shard_map/group/pallas_call | solution.py:476
  94.0 5.5 %last.1 = (f32[1024,1024]{1,0:T(8,128)}, f32[1024,1024]{1,0:T(8,128)}) custom-call(bf16[1024,512]{1,0:T(8,128)(2,1)S(1)} %get-tuple-element.8.th_ref, bf16[1024,512]{1,0:T(8,128)(2,1)S(1)} %get-tuple-element.9.tl_ref, f32[512,1024]{1,0:T(8,128)} %bitcast.6, f32[1024,1024]{1,0:T(8,128)S(1)} %get-tuple-element.10.f_ref, f32[512,1024]{1,0:T(8,128)S(1)} %get-tuple-element.11.tu_ref), custom_call_target="tpu_custom_call" | custom-call | flops 3221225472 | bytes 16777216 | tf_op jit(solution)/shard_map/last/pallas_call | solution.py:508

commit v4 on v3

--- a/solution.py
+++ b/solution.py
@@ -67,8 +67,17 @@
             for j in range(8):
                 for i in range(j + 1, 8):
                     r[i] = r[i] - l[i][j] * r[j]
-            for j in range(8):
-                r[j] = r[j] * inv[j]
+            scaled = [r[j] * inv[j] for j in range(8)]
+            if k + 1 < count:
+                v = rows[k + 1]
+                c = [lane_bcast(v, base + j) for j in range(8)]
+                for j in range(8):
+                    for i in range(j + 1, 8):
+                        c[i] = c[i] - l[i][j] * c[j]
+                acc = jnp.where(inside, 0.0, v)
+                p = [c[j] * scaled[j] for j in range(8)]
+                rows[k + 1] = acc - (((p[0] + p[1]) + (p[2] + p[3])) + ((p[4] + p[5]) + (p[6] + p[7])))
+            r = scaled
             for j in range(7, 0, -1):
                 for i in range(j):
                     r[i] = r[i] - l[j][i] * r[j]
@@ -76,11 +85,13 @@
             for i in range(1, 8):
                 out = jnp.where(subl == i, r[i], out)
             right[ti].append(jnp.where(seen, out, 0.0))
-            for m in range(k + 1, count):
-                v = rows[m]
-                acc = jnp.where(inside, 0.0, v)
-                p = [lane_bcast(v, base + j) * r[j] for j in range(8)]
-                rows[m] = acc - (((p[0] + p[1]) + (p[2] + p[3])) + ((p[4] + p[5]) + (p[6] + p[7])))
+            rest = {m: rows[m] for m in range(k + 2, count)}
+            accs = {m: jnp.where(inside, 0.0, v) for m, v in rest.items()}
+            for j in range(8):
+                for m, v in rest.items():
+                    accs[m] = accs[m] - lane_bcast(v, base + j) * r[j]
+            for m, v in accs.items():
+                rows[m] = v
     return [
         dot(jnp.concatenate(x, 0), jnp.concatenate(y, 0), ((0,), (0,)))
         for x, y in zip(left, right)
@@ -261,22 +272,23 @@
 
     invert_into([x1], lambda kb: None, fill_first)
     loads[2].wait()
-    w1[:, :e] = dot(x1[...], blk[0, 1])
-    strip = blk[0, 2, :, lo] - dot(blk[0, 1], w1[:, lo], tn)
-    mp[0] = strip[lo]
-    mp[1] = strip[hi]
-    mp[2] = blk[0, 2, hi, hi] - dot(blk[0, 1, :, hi], w1[:, hi], tn)
+    keep(x1h, x1l, x1[...])
+    keep(bh, bl, blk[0, 1].T)
+    w1[:, :e] = dot3((x1h[...], x1l[...]), split(blk[0, 1]))
+    ws = split(w1[:, :e])
+    strip = blk[0, 2] - dot3((bh[...], bl[...]), ws)
+    mp[0] = strip[lo, lo]
+    mp[1] = strip[hi, lo]
+    mp[2] = strip[hi, hi]
     z_m[0].start()
     x_b.wait_recv()
-    w1[:, e:] = dot(x1[...], blk[1, 1])
+    w1[:, e:] = dot3((x1h[...], x1l[...]), split(blk[1, 1]))
     part = jnp.where(is_left, blk[0, 1, :, lo], blk[1, 1, :, hi])
     cross = -dot(part, jnp.where(is_left, w1[:, e:], w1[:, :e]), tn)
     mp[3] = cross[:, lo]
     mp[4] = cross[:, hi]
     z_m[1].start()
 
-    keep(x1h, x1l, x1[...])
-    keep(bh, bl, blk[0, 1].T)
     for c in loads[6:8]:
         c.wait()
     loop(CHUNKS, lambda q: known(1, q))

time: 99.8 us -> 98.6 us (0.988)
  Pallas kernels: 98.9 us -> 97.6 us
    pallas_call x1, Pallas kernels: 93.4 us -> 92.1 us  [per_device(): pl.pallas_call(group_kernel, out_shape=(shape(full, cols), shape(2 * e, c...]
where the time goes in v4:
time: 98.6 us; the launch traced here: 98.4 us
  Pallas kernels  97.6 us (99%)
    pallas_call x1, Pallas kernels, per_device(): pl.pallas_call(group_kernel, out_shape=(shape(full, cols), shape(2 * e, c...  92.1 us
    pallas_call x1, Pallas kernels, per_device(): pl.pallas_call(last_kernel, out_shape=(shape(full, cols), shape(full, col...  5.51 us

profile of v4, /device:TPU:16, one launch (start us, length us, event | category | flops | bytes accessed | tf_op | source)
XLA Modules:
  0.0 98.4 jit_solution(17044030936821681228)
XLA Ops:
  0.6 92.1 %group.1 = (f32[1024,1024]{1,0:T(8,128)S(1)}, f32[512,1024]{1,0:T(8,128)S(1)}, bf16[1024,512]{1,0:T(8,128)(2,1)S(1)}, bf16[1024,512]{1,0:T(8,128)(2,1)S(1)}) custom-call(f32[1024,1024]{1,0:T(8,128)} %bitcast.4, f32[512,1024]{1,0:T(8,128)} %bitcast.5), custom_call_target="tpu_custom_call" | custom-call | flops 20000000000 | bytes 16777216 | tf_op jit(solution)/shard_map/group/pallas_call | solution.py:488
  92.8 5.5 %last.1 = (f32[1024,1024]{1,0:T(8,128)}, f32[1024,1024]{1,0:T(8,128)}) custom-call(bf16[1024,512]{1,0:T(8,128)(2,1)S(1)} %get-tuple-element.8.th_ref, bf16[1024,512]{1,0:T(8,128)(2,1)S(1)} %get-tuple-element.9.tl_ref, f32[512,1024]{1,0:T(8,128)} %bitcast.6, f32[1024,1024]{1,0:T(8,128)S(1)} %get-tuple-element.10.f_ref, f32[512,1024]{1,0:T(8,128)S(1)} %get-tuple-element.11.tu_ref), custom_call_target="tpu_custom_call" | custom-call | flops 3221225472 | bytes 16777216 | tf_op jit(solution)/shard_map/last/pallas_call | solution.py:520
